TPU v7x, 128 devices: a whole 4x4x4 slice. The times are simulated.
128 devices in a mesh: tm: 32 (over z, y, x_hi), space: 4 (over x_lo, core).
Axes of the slice: x: 4 (x_hi: 2, x_lo: 2; x = x_hi * 2 + x_lo), y: 4, z: 4, core: 2. Of those that a mesh axis runs over, the one named last changes fastest.
Arguments:
- frames: bfloat16 [512, 16, 64, 384], P('tm', 'space'), may hold values from -6 to 6
- token_ids: int32 [1, 512, 16, 64], P(None, 'tm', 'space'), may hold values from 0 to 1023
- action_ids: int32 [512], P('tm'), may hold values from 0 to 7
- token_table: bfloat16 [1024, 384], replicated, may hold values from -6 to 6
- action_table: bfloat16 [8, 384], replicated, may hold values from -3 to 3
- conv_weight: bfloat16 [3, 3, 384], replicated, may hold values from -1.796875 to 1.796875
- norm_gain: bfloat16 [384], replicated, may hold values from 0.5 to 1.5
- w_query: bfloat16 [384, 384], replicated, may hold values from -12 to 12
- w_key: bfloat16 [384, 384], replicated, may hold values from -12 to 12
- w_value: bfloat16 [384, 384], replicated, may hold values from -0.3125 to 0.3125
- w_out: bfloat16 [384, 384], replicated, may hold values from -0.625 to 0.625
Outputs:
- final_frames: bfloat16 [512, 16, 64, 384], P('tm', 'space')
All inputs are finite; a program needn't handle non-finite values.
Results may differ from a plain program's by a relative error of at most 0.0057.
Values may be sent and summed in bfloat16 or wider, within the bound.
No kernel may reach another device: no remote copies, remote signals or barrier semaphores. Data moves between devices by JAX's collectives and lax.ppermute only.
A program may use at most 192 MiB of HBM per device.

v0:
```python
import functools

import jax
import jax.numpy as jnp
from jax import lax
from jax.experimental import pallas as pl
from jax.experimental.pallas import tpu as pltpu
from jax.sharding import PartitionSpec as P

ACTIONS = 8
WINDOW = 16
ANCHORS = 4
BF = jnp.bfloat16
F32 = jnp.float32
LOG2E = 1.4426950408889634


def spread(ids_ref, hi_ref, lo_ref, frame0, count, pair):
    for f in range(count):
        at = slice(frame0 + f, frame0 + f + 1)
        row = jnp.concatenate([ids_ref[0, at, r, :] for r in pair], axis=1)
        wide = jnp.transpose(jnp.broadcast_to(row, (128, 128)))
        hi_ref[pl.ds(128 * f, 128), :] = (wide >> 7).astype(F32).astype(BF)
        lo_ref[pl.ds(128 * f, 128), :] = (wide & 127).astype(F32).astype(BF)


def lookup(hi, lo, table_ref):
    vocab = table_ref.shape[0]
    lane = lax.broadcasted_iota(jnp.int32, lo.shape, 1).astype(F32).astype(BF)
    at_lo = jnp.where(lo == lane, BF(1), BF(0))
    pieces = [jnp.where(hi == BF(k), at_lo, BF(0)) for k in range(vocab // 128)]
    return jnp.dot(jnp.concatenate(pieces, axis=1), table_ref[...], preferred_element_type=F32)


def conv_norm(load, cw_ref, gain_ref, put_mixed, get_mixed, put_normed):
    squares = None
    for j in range(3):
        at = slice(128 * j, 128 * j + 128)
        rows = [load(i, j) for i in range(3)]
        cols = rows[1].shape[0]
        index = lax.broadcasted_iota(jnp.int32, rows[1].shape, 0)

        def part(c):
            return sum(rows[i] * cw_ref[i, c : c + 1, at].astype(F32) for i in range(3))

        mixed = rows[1] + part(1)
        mixed += jnp.where(index == 0, F32(0), pltpu.roll(part(0), 1, 0))
        mixed += jnp.where(index == cols - 1, F32(0), pltpu.roll(part(2), cols - 1, 0))
        put_mixed(j, mixed)
        squares = mixed * mixed if squares is None else squares + mixed * mixed
    scale = lax.rsqrt(jnp.sum(squares, axis=-1, keepdims=True) * F32(1 / 384) + 1e-06)
    for j in range(3):
        put_normed(j, (get_mixed(j) * scale * gain_ref[:, 128 * j : 128 * j + 128].astype(F32)).astype(BF))


def embed_kernel(
    frame0, count, pair, ids_ref, act_ref, table_ref, top_ref, low_ref, a_ref, b_ref, hi, lo
):
    f = pl.program_id(0)

    @pl.when(f == 0)
    def _():
        spread(ids_ref, hi, lo, frame0, count, pair)

    step = top_ref.shape[0]
    at = pl.ds(pl.multiple_of(128 * step * f, 128), 128 * step)
    token = lookup(hi[at, :], lo[at, :], table_ref)
    for i in range(step):
        act = act_ref[pl.ds(frame0 + step * f + i, 1), :]
        for k, ref, to in ((0, top_ref, a_ref), (1, low_ref, b_ref)):
            t = token[128 * i + 64 * k : 128 * i + 64 * k + 64]
            to[i] = (ref[i, 0].astype(F32) + t + act).astype(BF)


def finish(frame0, step, three, cw_ref, gain_ref, held, wins, mixed_ref, anc_ref, rows):
    f0 = pl.program_id(0) * step
    if held:

        @pl.when(f0 == 0)
        def _():
            for old, new in zip(held, wins):
                new[pl.ds(0, frame0 - 1)] = old[...]

    for i in range(step):
        f = frame0 + f0 + i
        for k, win_ref in enumerate(wins):
            def put_mixed(j, value):
                mixed_ref[i, k, :, 128 * j : 128 * j + 128] = value

            def get_mixed(j):
                return mixed_ref[i, k, :, 128 * j : 128 * j + 128]

            def put_normed(j, value):
                at = slice(128 * j, 128 * j + 128)
                win_ref[jnp.maximum(f - 1, 0), :, at] = value
                if anc_ref is not None:
                    anc_ref[f, rows[k], :, at] = value

            conv_norm(
                functools.partial(three, i, k), cw_ref, gain_ref, put_mixed, get_mixed, put_normed
            )


def inner_kernel(
    frame0, count, ids_ref, act_ref, table_ref, top_ref, low_ref, e0_ref, e3_ref, cw_ref, gain_ref,
    *rest
):
    held = rest[:2] if frame0 else ()
    rest = rest[len(held) :]
    e1_ref, e2_ref, win_a_ref, win_b_ref, mixed_ref = rest[:5]
    anc_ref = None if frame0 else rest[5]
    hi, lo = rest[-2:]
    embed_kernel(
        frame0, count, (1, 2), ids_ref, act_ref, table_ref, top_ref, low_ref, e1_ref, e2_ref, hi, lo
    )
    rows = (e0_ref, e1_ref, e2_ref, e3_ref)

    def three(i, k, r, j):
        return rows[k + r][i, :, 128 * j : 128 * j + 128].astype(F32)

    finish(
        frame0, top_ref.shape[0], three, cw_ref, gain_ref, held, (win_a_ref, win_b_ref),
        mixed_ref, anc_ref, (0, 1),
    )


def edge_kernel(
    frame0, last, flag_ref, up_ref, e0_ref, e1_ref, e2_ref, e3_ref, down_ref, cw_ref, gain_ref, *rest
):
    held = rest[:2] if frame0 else ()
    rest = rest[len(held) :]
    win_a_ref, win_b_ref, mixed_ref = rest[:3]
    anc_ref = None if frame0 else rest[3]
    keep = [jnp.where(flag_ref[0] != k, F32(1), F32(0)) for k in (0, last)]
    rows = ((up_ref, e0_ref, e1_ref), (e2_ref, e3_ref, down_ref))

    def three(i, k, r, j):
        row = rows[k][r][i, :, 128 * j : 128 * j + 128].astype(F32)
        return row * keep[k] if r == 2 * k else row

    finish(
        frame0, e0_ref.shape[0], three, cw_ref, gain_ref, held, (win_a_ref, win_b_ref),
        mixed_ref, anc_ref, (0, 1),
    )


def attend_kernel(
    first_ref, own0_ref, own_ref, halo_ref, anc_ref, mix_a_ref, mix_b_ref, wqkv_ref,
    wo_ref, *rest
):
    out_ref, qs, ks, vs, hk, hv, ak, av, att, bias = rest[-10:]
    D = 384
    cols = 64
    first = first_ref[0]
    pitch = cols + 1

    def put(to, row0, value, every=cols, gap=pitch):
        for j in range(3):
            for i in range(value.shape[0] // every):
                piece = value[i * every : i * every + every, 128 * j : 128 * j + 128]
                to[j, pl.ds(row0 + i * gap, every), :] = piece

    def qkv(x, row0, q_to, k_to, v_to):
        for i, to in enumerate((q_to, k_to, v_to)):
            if to is not None:
                w = wqkv_ref[:, D * i : D * i + D]
                put(to, row0, jnp.dot(x, w, preferred_element_type=F32))

    qkv(own0_ref[0, 0], 0, qs, ks, vs)
    zero = jnp.zeros((cols, D), F32)
    put(hk, 0, zero)
    put(hv, 0, zero)

    @pl.loop(0, 3)
    def _(i):
        x = own_ref[pl.ds(5 * i, 5)].reshape(5 * cols, D)
        qkv(x, pitch + i * 5 * pitch, qs, ks, vs)
        x = halo_ref[pl.ds(5 * i, 5)].reshape(5 * cols, D)
        qkv(x, pitch + i * 5 * pitch, None, hk, hv)

    qkv(anc_ref[:, 0].reshape(ANCHORS * cols, D), 0, None, ak, av)
    for u in range(ANCHORS, 8):
        put(ak, u * pitch, zero)
        put(av, u * pitch, zero)

    row = lax.broadcasted_iota(jnp.int32, (64, 128), 0)
    col = lax.broadcasted_iota(jnp.int32, (64, 128), 1)
    same = ((row // 8) % 4) == (col // 32)
    key = col % 32
    for half in range(2):
        t = row % 8 + 8 * half
        tail = jnp.where(key < 24, key - 16, 0)
        if half == 0:
            before = key >= t + 1
            before = before & (key < 16)
            own = (key >= 16) & (key < 24) & (tail <= t)
        else:
            own = (key < 16) & (key <= t)
            before = (key >= 16) & (key < 24) & (tail + 8 >= t + 1)
        before = before & (first >= 16)
        anchor = (key >= 24) & (key < 28) & (key - 24 < first + t - (WINDOW - 1))
        ok = same & (own | before | anchor)
        bias[half] = jnp.where(ok, F32(0), F32(-1e30))

    lane = lax.broadcasted_iota(jnp.int32, (32, 128), 1)
    low = lane < 64
    c = F32(LOG2E / 8.0)

    GROUPS = 4

    @pl.loop(0, cols // (4 * GROUPS))
    def _(g):
        first_col = g * 4 * GROUPS

        def eight(ref, frame0, p, j):
            return ref[j, pl.ds(frame0 * pitch + first_col + p, 8, stride=pitch), :]

        def scores(group, j):
            qh, kh, vh = [[], []], [[], []], [[], []]
            for p in range(4 * group, 4 * group + 4):
                for half in range(2):
                    qh[half].append(eight(qs, 8 * half, p, j))
                for src_h, src_o, src_a, to in ((hk, ks, ak, kh), (hv, vs, av, vh)):
                    a_lo, a_hi = eight(src_h, 0, p, j), eight(src_h, 8, p, j)
                    b_lo, b_hi = eight(src_o, 0, p, j), eight(src_o, 8, p, j)
                    anc = eight(src_a, 0, p, j)
                    to[0] += [a_lo, a_hi, b_lo, anc]
                    to[1] += [b_lo, b_hi, a_hi, anc]
            found = []
            for half in range(2):
                q = jnp.concatenate(qh[half], axis=0).astype(BF)
                k = jnp.concatenate(kh[half], axis=0).astype(BF)
                v = jnp.concatenate(vh[half], axis=0).astype(BF)
                nil = jnp.zeros_like(q)
                qq = jnp.concatenate([jnp.where(low, q, nil), jnp.where(low, nil, q)], axis=0)
                s = lax.dot_general(
                    qq, k, (((1,), (1,)), ((), ())), preferred_element_type=F32
                )
                found.append((group, j, half, s, v))
            return found

        def values(group, j, half, s, v):
            s = s * c + bias[half]
            e = jnp.exp2(s - jnp.max(s, axis=-1, keepdims=True))
            total = jnp.sum(e, axis=-1, keepdims=True)
            o = jnp.dot(e.astype(BF), v, preferred_element_type=F32) / total
            o = jnp.where(low, o[:32], o[32:])
            for p in range(4):
                at = pl.multiple_of((first_col + 4 * group + p) * 16 + 8 * half, 8)
                att[pl.ds(at, 8), pl.ds(128 * j, 128)] = o[8 * p : 8 * p + 8]

        found = []
        for group in range(GROUPS):
            for j in range(3):
                found += scores(group, j)
        for one in found:
            values(*one)

    @pl.loop(0, 4)
    def _(i):
        x = att[pl.ds(i * 256, 256), :].astype(BF)
        put(qs, i * 16 * 17, jnp.dot(x, wo_ref[...], preferred_element_type=F32), 16, 17)

    t0 = 0
    for mixed_ref in (mix_a_ref, mix_b_ref):

        @pl.loop(0, mixed_ref.shape[0])
        def _(i, t0=t0, mixed_ref=mixed_ref):
            t = t0 + i
            for j in range(3):
                got = qs[j, pl.ds(t, cols, stride=17), :]
                out_ref[t, 0, :, pl.ds(128 * j, 128)] = (
                    mixed_ref[i, 0, :, pl.ds(128 * j, 128)] + got
                ).astype(BF)

        t0 += mixed_ref.shape[0]


def whole(shape):
    return pl.BlockSpec(shape, lambda *_: (0,) * len(shape), pipeline_mode=pl.Buffered(1))


def on_device(
    frames, token_ids, action_ids, token_table, action_table, conv_weight, norm_gain,
    w_query, w_key, w_value, w_out,
):
    F, R, C, D = frames.shape
    tm, sp = lax.axis_index("tm"), lax.axis_index("space")
    n_tm, n_sp = lax.axis_size("tm"), lax.axis_size("space")
    onehot = (action_ids[:, None] == jnp.arange(ACTIONS, dtype=jnp.int32)[None, :]).astype(BF)
    act = jnp.dot(onehot, action_table, preferred_element_type=F32)
    cw, gain = conv_weight, norm_gain.reshape(1, D)
    wqkv = jnp.concatenate([w_query, w_key, w_value], axis=1)

    up_pairs = [(i, i + 1) for i in range(n_sp - 1)]
    down_pairs = [(j, i) for i, j in up_pairs]
    step = 2
    parts = ((0, 4), (4, 12))
    table_specs = [whole((1, F, R, C)), whole((F, D)), whole(token_table.shape)]
    conv_specs = [whole((3, 3, D)), whole((1, D))]

    def row_of(r, f0=0):
        return pl.BlockSpec((step, 1, C, D), lambda f, *_: (f0 // step + f, r, 0, 0))

    line = pl.BlockSpec((step, C, D), lambda f, *_: (f, 0, 0))
    pair = pl.BlockSpec((step, 2, C, D), lambda f, *_: (f, 0, 0, 0))

    def shape(n, *k):
        return jax.ShapeDtypeStruct((n, *k, C, D), BF)

    def cost(us):
        return pl.CostEstimate(flops=int(us * 4e8), bytes_accessed=int(us * 1e5), transcendentals=0)

    flags = sp.astype(jnp.int32).reshape(1)
    edges = []
    for (f0, n) in parts:
        e0, e3 = pl.pallas_call(
            functools.partial(embed_kernel, f0, n, (0, R - 1)),
            grid=(n // step,),
            in_specs=table_specs + [row_of(0, f0), row_of(R - 1, f0)],
            out_specs=[line] * 2,
            out_shape=[shape(n)] * 2,
            scratch_shapes=[pltpu.VMEM((n * 2 * C, 128), BF)] * 2,
            cost_estimate=cost(n / 2),
            name="embed",
        )(token_ids, act, token_table, frames, frames)
        up = lax.ppermute(e3, "space", up_pairs)
        down = lax.ppermute(e0, "space", down_pairs)
        edges.append((e0, e3, up, down))

    def win_outs(f0, n):
        so_far = f0 + n - 1
        return (
            [shape(so_far)] * 2 + [jax.ShapeDtypeStruct((n, 2, C, D), F32)],
            [whole((so_far, C, D))] * 2 + [pair],
        )

    inner, mids, mixed12 = [], [], []
    for p, (f0, n) in enumerate(parts):
        shapes, specs = win_outs(f0, n)
        in_specs = table_specs + [row_of(1, f0), row_of(2, f0), line, line] + conv_specs
        operands = [token_ids, act, token_table, frames, frames, *edges[p][:2], cw, gain]
        if f0:
            in_specs += [whole((f0 - 1, C, D))] * 2
            operands += inner[-1][:2]
        else:
            shapes = shapes + [shape(ANCHORS, 2)]
            specs = specs + [whole((ANCHORS, 2, C, D))]
        e1, e2, *rest = pl.pallas_call(
            functools.partial(inner_kernel, f0, n),
            grid=(n // step,),
            in_specs=in_specs,
            out_specs=[line] * 2 + specs,
            out_shape=[shape(n)] * 2 + shapes,
            scratch_shapes=[pltpu.VMEM((n * 2 * C, 128), BF)] * 2,
            cost_estimate=cost(n),
            name="inner",
        )(*operands)
        mids.append((e1, e2))
        inner.append(rest)
        mixed12.append(rest[2])

    outer, mixed03 = [], []
    for p, (f0, n) in enumerate(parts):
        shapes, specs = win_outs(f0, n)
        e0, e3, up, down = edges[p]
        in_specs = [line] * 6 + conv_specs
        operands = [flags, up, e0, *mids[p], e3, down, cw, gain]
        if f0:
            in_specs += [whole((f0 - 1, C, D))] * 2
            operands += outer[-1][:2]
        else:
            shapes = shapes + [shape(ANCHORS, 2)]
            specs = specs + [whole((ANCHORS, 2, C, D))]
        rest = pl.pallas_call(
            functools.partial(edge_kernel, f0, n_sp - 1),
            grid_spec=pltpu.PrefetchScalarGridSpec(
                num_scalar_prefetch=1,
                grid=(n // step,),
                in_specs=in_specs,
                out_specs=specs,
            ),
            out_shape=shapes,
            cost_estimate=cost(n),
            name="edge",
        )(*operands)
        outer.append(rest)
        mixed03.append(rest[2])

    own_anchors = {"a": inner[0][3], "b": outer[0][3]}
    held = dict(own_anchors)
    have = {k: [0] for k in range(n_sp)}
    z, y = tm // 8, tm // 2 % 4
    even = sp % 2 == 0
    a, b = jnp.where(even, z, y), jnp.where(even, y, z)
    fresh = [tm == 1, (a == 2) & (b == 0), (a % 2 == 1) & (b == 0), b == 3, b == 2, b == 1]

    def moves_of(n, k, holders):
        a_by, b_by = (8, 2) if k % 2 == 0 else (2, 8)
        if n == 0:
            return [(t, t + 1) for t in holders]
        if n == 1:
            return [(t, t + 2 * a_by) for t in holders]
        if n == 2:
            return [(t, t + 3 * a_by if t // a_by % 4 == 0 else t - a_by) for t in holders]
        if n == 3:
            return [(t, t + 3 * b_by) for t in holders]
        return [(t, t - b_by) for t in holders if t // b_by % 4 == 7 - n]

    for n in range(6):
        moves = [(t, to, k) for k in range(n_sp) for t, to in moves_of(n, k, have[k])]
        for _, to, k in moves:
            have[k] = have[k] + [to]
        pairs = [(t * n_sp + k, to * n_sp + k) for t, to, k in moves]
        for tree in "ab":
            got = lax.ppermute(held[tree], ("tm", "space"), pairs)
            held[tree] = jnp.where(fresh[n], got, held[tree])

    shift = [(i, i + 1) for i in range(n_tm - 1)]
    wins = {1: inner[-1][0], 2: inner[-1][1], 0: outer[-1][0], 3: outer[-1][1]}
    halos = {}
    for r in (1, 2, 0, 3):
        halos[r] = lax.ppermute(wins[r], "tm", shift)

    first = (tm * F).astype(jnp.int32).reshape(1)
    out = None
    for r in (1, 2, 0, 3):
        if r in (1, 2):
            k, mixed, tree = r - 1, mixed12, "a"
        else:
            k, mixed, tree = r // 3, mixed03, "b"
        one = dict(pipeline_mode=pl.Buffered(1))
        in_specs = [
            pl.BlockSpec((1, 1, C, D), lambda i, *_, k=k: (0, k, 0, 0), **one),
            whole((F - 1, C, D)),
            whole((F - 1, C, D)),
            pl.BlockSpec((ANCHORS, 1, C, D), lambda i, *_, k=k: (0, k, 0, 0), **one),
        ]
        in_specs += [
            pl.BlockSpec((n, 1, C, D), lambda i, *_, k=k: (0, k, 0, 0), **one) for _, n in parts
        ]
        in_specs += [whole((D, 3 * D)), whole((D, D))]
        operands = [
            first, own_anchors[tree], wins[r], halos[r], held[tree], *mixed, wqkv, w_out
        ]
        aliases = {}
        if out is not None:
            in_specs.append(pl.BlockSpec(memory_space=pl.ANY))
            operands.append(out)
            aliases = {len(operands) - 1: 0}
        out = pl.pallas_call(
            attend_kernel,
            grid_spec=pltpu.PrefetchScalarGridSpec(
                num_scalar_prefetch=1,
                grid=(1,),
                in_specs=in_specs,
                out_specs=pl.BlockSpec((F, 1, C, D), lambda i, *_, r=r: (0, r, 0, 0), **one),
                scratch_shapes=[pltpu.VMEM((3, 17 * (C + 1), 128), F32)] * 5
                + [pltpu.VMEM((3, 8 * (C + 1), 128), F32)] * 2
                + [pltpu.VMEM((F * C, D), F32), pltpu.VMEM((2, 64, 128), F32)],
            ),
            out_shape=jax.ShapeDtypeStruct((F, R, C, D), BF),
            input_output_aliases=aliases,
            cost_estimate=cost(10),
            name="attend",
        )(*operands)
    return out


def solution(mesh):
    in_specs = (
        P("tm", "space", None, None),
        P(None, "tm", "space", None),
        P("tm"),
        P(), P(), P(), P(), P(), P(), P(), P(),
    )
    out_specs = P("tm", "space", None, None)

    return jax.shard_map(
        on_device, mesh=mesh, in_specs=in_specs, out_specs=out_specs, check_vma=False
    )
```

profile of v0, /device:TPU:22, one launch (start us, length us, event | category | flops | bytes accessed | tf_op | source)
XLA Modules:
  0.0 153.0 jit_solution(3970179713941979753)
XLA Ops:
  1.2 1.4 fusion.act_ref
  2.7 3.1 %embed.2 = (bf16[4,64,384]{2,1,0:T(8,128)(2,1)}, bf16[4,64,384]{2,1,0:T(8,128)(2,1)}) custom-call(s32[1,16,4,64]{3,2,1,0:T(4,128)} %ids_ref.7, f32[16,384]{1,0:T(8,128)} %fusion.act_ref, bf16[1024,384]{1,0:T(8,128)(2,1)} %table_ref.7, bf16[16,4,64,384]{3,2,1,0:T(8,128)(2,1)} %low_ref.7, bf16[16,4,64,384]{3,2,1,0:T(8,128)(2,1)} %low_ref.7), custom_call_target="tpu_custom_call" | custom-call | flops 800000000 | bytes 200000 | tf_op jit(solution)/shard_map/embed/pallas_call | solution.py:317
  5.8 4.6 %inner.2 = (bf16[4,64,384]{2,1,0:T(8,128)(2,1)}, bf16[4,64,384]{2,1,0:T(8,128)(2,1)}, bf16[3,64,384]{2,1,0:T(8,128)(2,1)}, bf16[3,64,384]{2,1,0:T(8,128)(2,1)}, ...) custom-call(s32[1,16,4,64]{3,2,1,0:T(4,128)} %ids_ref.7, f32[16,384]{1,0:T(8,128)} %fusion.act_ref, ...), custom_call_target="tpu_custom_call" | custom-call | flops 1600000000 | bytes 400000 | tf_op jit(solution)/shard_map/inner/pallas_call | solution.py:349
  11.2 1.9 %collective-permute-start = (bf16[4,64,384]{2,1,0:T(8,128)(2,1)S(1)}, bf16[4,64,384]{2,1,0:T(8,128)(2,1)S(1)}, u32[]{:S(2)}, u32[]{:S(2)}) collective-permute-start(bf16[4,64,384]{2,1,0:T(8,128)(2,1)S(1)} %copy-done.6), channel_id=1, source_target_pairs={{0,1},{1,2},{2,3},{4,5},{5,6},{6,7},{8,9},{9,10},{10,11},{12,13},{... | collective-permute-start | bytes 589832 | tf_op jit(solution)/shard_map/ppermute | solution.py:327
  13.1 3.6 %collective-permute-start.1 = (bf16[4,64,384]{2,1,0:T(8,128)(2,1)S(1)}, bf16[4,64,384]{2,1,0:T(8,128)(2,1)S(1)}, u32[]{:S(2)}, u32[]{:S(2)}) collective-permute-start(bf16[4,64,384]{2,1,0:T(8,128)(2,1)S(1)} %copy-done.5), channel_id=1, source_target_pairs={{1,0},{2,1},{3,2},{5,4},{6,5},{7,6},{9,8},{10,9},{11,10},{13,12},{... | collective-permute-start | bytes 589832 | tf_op jit(solution)/shard_map/ppermute | solution.py:328
  16.8 1.4 collective-permute-done.up_ref
  18.2 1.8 %collective-permute-done.1.down_ref = bf16[4,64,384]{2,1,0:T(8,128)(2,1)S(1)} collective-permute-done((bf16[4,64,384]{2,1,0:T(8,128)(2,1)S(1)}, bf16[4,64,384]{2,1,0:T(8,128)(2,1)S(1)}, u32[]{:S(2)}, u32[]{:S(2)}) %collective-permute-start.1) | collective-permute-done | bytes 196640 | tf_op jit(solution)/shard_map/ppermute | solution.py:328
  20.6 3.1 %edge.2 = (bf16[3,64,384]{2,1,0:T(8,128)(2,1)}, bf16[3,64,384]{2,1,0:T(8,128)(2,1)}, f32[4,2,64,384]{3,2,1,0:T(8,128)}, bf16[4,2,64,384]{3,2,1,0:T(8,128)(2,1)}) custom-call(s32[1]{0:T(128)} %bitcast.1.flag_ref, bf16[4,64,384]{2,1,0:T(8,128)(2,1)} %copy-done.9, bf16[4,64,384]{2,1,0:T(8,128)(2,1)} %get-tuple-element.28.e0_ref, ...), custom_call_target="tpu_custom_call" | custom-call | flops 1600000000 | bytes 400000 | tf_op jit(solution)/shard_map/edge/pallas_call | solution.py:375
  27.8 6.3 %embed.3 = (bf16[12,64,384]{2,1,0:T(8,128)(2,1)}, bf16[12,64,384]{2,1,0:T(8,128)(2,1)}) custom-call(s32[1,16,4,64]{3,2,1,0:T(4,128)} %ids_ref.7, f32[16,384]{1,0:T(8,128)} %fusion.act_ref, bf16[1024,384]{1,0:T(8,128)(2,1)} %table_ref.7, bf16[16,4,64,384]{3,2,1,0:T(8,128)(2,1)} %low_ref.7, bf16[16,4,64,384]{3,2,1,0:T(8,128)(2,1)} %low_ref.7), custom_call_target="tpu_custom_call" | custom-call | flops 2400000000 | bytes 600000 | tf_op jit(solution)/shard_map/embed/pallas_call | solution.py:317
  34.1 6.7 %collective-permute-start.2 = (bf16[12,64,384]{2,1,0:T(8,128)(2,1)}, bf16[12,64,384]{2,1,0:T(8,128)(2,1)}, u32[]{:S(2)}, u32[]{:S(2)}) collective-permute-start(bf16[12,64,384]{2,1,0:T(8,128)(2,1)} %get-tuple-element.32.e3_ref), channel_id=1, source_target_pairs={{0,1},{1,2},{2,3},{4,5},{5,6},{6,7},{8,9},{9,10},{10,11},{12,13},{... | collective-permute-start | bytes 1769480 | tf_op jit(solution)/shard_map/ppermute | solution.py:327
  40.7 7.2 %collective-permute-start.3 = (bf16[12,64,384]{2,1,0:T(8,128)(2,1)}, bf16[12,64,384]{2,1,0:T(8,128)(2,1)}, u32[]{:S(2)}, u32[]{:S(2)}) collective-permute-start(bf16[12,64,384]{2,1,0:T(8,128)(2,1)} %get-tuple-element.33.e0_ref), channel_id=1, source_target_pairs={{1,0},{2,1},{3,2},{5,4},{6,5},{7,6},{9,8},{10,9},{11,10},{13,12},{... | collective-permute-start | bytes 1769480 | tf_op jit(solution)/shard_map/ppermute | solution.py:328
  49.5 9.4 %inner.3 = (bf16[12,64,384]{2,1,0:T(8,128)(2,1)}, bf16[12,64,384]{2,1,0:T(8,128)(2,1)}, bf16[15,64,384]{2,1,0:T(8,128)(2,1)}, bf16[15,64,384]{2,1,0:T(8,128)(2,1)}, f32[12,2,64,384]{3,2,1,0:T(8,128)}) custom-call(s32[1,16,4,64]{3,2,1,0:T(4,128)} %ids_ref.7, f32[16,384]{1,0:T(8,128)} %fusion.act_ref, bf16[1024,384]{1,0:T(8,128)(2,1)} %table_ref.7, ...), custom_call_target="tpu_custom_call" | custom-call | flops 4800000000 | bytes 1200000 | tf_op jit(solution)/shard_map/inner/pallas_call | solution.py:349
  58.9 2.1 %collective-permute-start.19 = (bf16[15,64,384]{2,1,0:T(8,128)(2,1)}, bf16[15,64,384]{2,1,0:T(8,128)(2,1)}, u32[]{:S(2)}, u32[]{:S(2)}) collective-permute-start(bf16[15,64,384]{2,1,0:T(8,128)(2,1)} %get-tuple-element.48.own_ref), channel_id=1, source_target_pairs={{0,4},{4,8},{8,12},{12,16},{16,20},{20,24},{24,28},{28,32},{32,36}... | collective-permute-start | bytes 2211848 | tf_op jit(solution)/shard_map/ppermute | solution.py:423
  62.6 1.3 collective-permute-start.17
  65.5 18.1 %collective-permute-start.12 = (bf16[15,64,384]{2,1,0:T(8,128)(2,1)S(1)}, bf16[15,64,384]{2,1,0:T(8,128)(2,1)}, u32[]{:S(2)}, u32[]{:S(2)}) collective-permute-start(bf16[15,64,384]{2,1,0:T(8,128)(2,1)S(1)} %copy-done.7), channel_id=1, source_target_pairs={{0,4},{4,8},{8,12},{12,16},{16,20},{20,24},{24,28},{28,32},{32,36}... | collective-permute-start | bytes 2211848 | tf_op jit(solution)/shard_map/ppermute | solution.py:423
  85.1 1.3 collective-permute-start.18
  86.4 7.0 %edge.3 = (bf16[15,64,384]{2,1,0:T(8,128)(2,1)}, bf16[15,64,384]{2,1,0:T(8,128)(2,1)}, f32[12,2,64,384]{3,2,1,0:T(8,128)}) custom-call(s32[1]{0:T(128)} %bitcast.1.flag_ref, bf16[12,64,384]{2,1,0:T(8,128)(2,1)} %collective-permute-done.2.up_ref, bf16[12,64,384]{2,1,0:T(8,128)(2,1)} %get-tuple-element.33.e0_ref, ...), custom_call_target="tpu_custom_call" | custom-call | flops 4800000000 | bytes 1200000 | tf_op jit(solution)/shard_map/edge/pallas_call | solution.py:375
  93.4 1.9 %collective-permute-start.11 = (bf16[15,64,384]{2,1,0:T(8,128)(2,1)}, bf16[15,64,384]{2,1,0:T(8,128)(2,1)}, u32[]{:S(2)}, u32[]{:S(2)}) collective-permute-start(bf16[15,64,384]{2,1,0:T(8,128)(2,1)} %get-tuple-element.43.own_ref), channel_id=1, source_target_pairs={{0,4},{4,8},{8,12},{12,16},{16,20},{20,24},{24,28},{28,32},{32,36}... | collective-permute-start | bytes 2211848 | tf_op jit(solution)/shard_map/ppermute | solution.py:423
  95.4 6.9 %collective-permute-start.4 = (bf16[15,64,384]{2,1,0:T(8,128)(2,1)}, bf16[15,64,384]{2,1,0:T(8,128)(2,1)S(1)}, u32[]{:S(2)}, u32[]{:S(2)}) collective-permute-start(bf16[15,64,384]{2,1,0:T(8,128)(2,1)} %get-tuple-element.40.own_ref), channel_id=1, source_target_pairs={{0,4},{4,8},{8,12},{12,16},{16,20},{20,24},{24,28},{28,32},{32,36}... | collective-permute-start | bytes 2211848 | tf_op jit(solution)/shard_map/ppermute | solution.py:423
  102.4 2.1 %collective-permute-start.10 = (bf16[4,2,64,384]{3,2,1,0:T(8,128)(2,1)S(1)}, bf16[4,2,64,384]{3,2,1,0:T(8,128)(2,1)S(1)}, u32[]{:S(2)}, u32[]{:S(2)}) collective-permute-start(bf16[4,2,64,384]{3,2,1,0:T(8,128)(2,1)S(1)} %broadcast_select_fusion.9), channel_id=1, source_target_pairs={{16,8},{20,12},{80,72},{84,76},{112,104},{116,108},{48,40},{52,44}... | collective-permute-start | bytes 1179656 | tf_op jit(solution)/shard_map/ppermute | solution.py:416
  105.3 11.5 %attend.4.rest_0_ = bf16[16,4,64,384]{3,2,1,0:T(8,128)(2,1)} custom-call(s32[1]{0:T(128)} %bitcast.first_ref, bf16[4,2,64,384]{3,2,1,0:T(8,128)(2,1)} %get-tuple-element.44.own0_ref, bf16[15,64,384]{2,1,0:T(8,128)(2,1)} %get-tuple-element.48.own_ref, bf16[15,64,384]{2,1,0:T(8,128)(2,1)} %collective-permute-done.19.halo_ref, ...), custom_call_target="tpu_custom_call" | custom-call | flops 4000000000 | bytes 1000000 | tf_op jit(solution)/shard_map/attend/pallas_call | solution.py:451
  116.8 11.5 %attend.5.rest_0_ = bf16[16,4,64,384]{3,2,1,0:T(8,128)(2,1)} custom-call(s32[1]{0:T(128)} %bitcast.first_ref, bf16[4,2,64,384]{3,2,1,0:T(8,128)(2,1)} %get-tuple-element.44.own0_ref, bf16[15,64,384]{2,1,0:T(8,128)(2,1)} %get-tuple-element.45.own_ref, bf16[15,64,384]{2,1,0:T(8,128)(2,1)} %collective-permute-done.12.halo_ref, ...), custom_call_target="tpu_custom_call", output_to_operand_aliasing={{}: (9, {})} | custom-call | flops 4000000000 | bytes 1000000 | tf_op jit(solution)/shard_map/attend/pallas_call | solution.py:451
  129.2 11.5 %attend.6.rest_0_ = bf16[16,4,64,384]{3,2,1,0:T(8,128)(2,1)} custom-call(s32[1]{0:T(128)} %bitcast.first_ref, bf16[4,2,64,384]{3,2,1,0:T(8,128)(2,1)} %get-tuple-element.31.own0_ref, bf16[15,64,384]{2,1,0:T(8,128)(2,1)} %get-tuple-element.43.own_ref, bf16[15,64,384]{2,1,0:T(8,128)(2,1)} %collective-permute-done.11.halo_ref, ...), custom_call_target="tpu_custom_call", output_to_operand_aliasing={{}: (9, {})} | custom-call | flops 4000000000 | bytes 1000000 | tf_op jit(solution)/shard_map/attend/pallas_call | solution.py:451
  141.5 11.5 %attend.7 = bf16[16,4,64,384]{3,2,1,0:T(8,128)(2,1)} custom-call(s32[1]{0:T(128)} %bitcast.first_ref, bf16[4,2,64,384]{3,2,1,0:T(8,128)(2,1)} %get-tuple-element.31.own0_ref, bf16[15,64,384]{2,1,0:T(8,128)(2,1)} %get-tuple-element.40.own_ref, bf16[15,64,384]{2,1,0:T(8,128)(2,1)} %copy-done.8, ...), custom_call_target="tpu_custom_call", output_to_operand_aliasing={{}: (9, {})} | custom-call | flops 4000000000 | bytes 1000000 | tf_op jit(solution)/shard_map/attend/pallas_call | solution.py:451
  (65 shorter events, 15.4 us)
Async XLA Ops:
  5.8 7.3 %copy-start.5 = (bf16[4,64,384]{2,1,0:T(8,128)(2,1)S(1)}, bf16[4,64,384]{2,1,0:T(8,128)(2,1)}, u32[]{:S(2)}) copy-start(bf16[4,64,384]{2,1,0:T(8,128)(2,1)} %get-tuple-element.28.e0_ref) | copy-start | bytes 589828
  10.3 14.1 %copy-start.1 = (bf16[4,2,64,384]{3,2,1,0:T(8,128)(2,1)S(1)}, bf16[4,2,64,384]{3,2,1,0:T(8,128)(2,1)}, u32[]{:S(2)}) copy-start(bf16[4,2,64,384]{3,2,1,0:T(8,128)(2,1)} %get-tuple-element.44.own0_ref) | copy-start | bytes 1179652
  10.3 14.1 %collective-permute-start.13 = (bf16[4,2,64,384]{3,2,1,0:T(8,128)(2,1)}, bf16[4,2,64,384]{3,2,1,0:T(8,128)(2,1)S(1)}, u32[]{:S(2)}, u32[]{:S(2)}) collective-permute-start(bf16[4,2,64,384]{3,2,1,0:T(8,128)(2,1)} %get-tuple-element.44.own0_ref), channel_id=1, source_target_pairs={{0,4},{1,5},{2,6},{3,7}} | collective-permute-start | bytes 1179656 | tf_op jit(solution)/shard_map/ppermute | solution.py:416
  11.2 7.0 %collective-permute-start = (bf16[4,64,384]{2,1,0:T(8,128)(2,1)S(1)}, bf16[4,64,384]{2,1,0:T(8,128)(2,1)S(1)}, u32[]{:S(2)}, u32[]{:S(2)}) collective-permute-start(bf16[4,64,384]{2,1,0:T(8,128)(2,1)S(1)} %copy-done.6), channel_id=1, source_target_pairs={{0,1},{1,2},{2,3},{4,5},{5,6},{6,7},{8,9},{9,10},{10,11},{12,13},{... | collective-permute-start | bytes 589832 | tf_op jit(solution)/shard_map/ppermute | solution.py:327
  13.1 6.8 %collective-permute-start.1 = (bf16[4,64,384]{2,1,0:T(8,128)(2,1)S(1)}, bf16[4,64,384]{2,1,0:T(8,128)(2,1)S(1)}, u32[]{:S(2)}, u32[]{:S(2)}) collective-permute-start(bf16[4,64,384]{2,1,0:T(8,128)(2,1)S(1)} %copy-done.5), channel_id=1, source_target_pairs={{1,0},{2,1},{3,2},{5,4},{6,5},{7,6},{9,8},{10,9},{11,10},{13,12},{... | collective-permute-start | bytes 589832 | tf_op jit(solution)/shard_map/ppermute | solution.py:328
  23.7 1.5 collective-permute-start.5
  24.5 2.5 %collective-permute-start.14 = (bf16[4,2,64,384]{3,2,1,0:T(8,128)(2,1)S(1)}, bf16[4,2,64,384]{3,2,1,0:T(8,128)(2,1)S(1)}, u32[]{:S(2)}, u32[]{:S(2)}) collective-permute-start(bf16[4,2,64,384]{3,2,1,0:T(8,128)(2,1)S(1)} %broadcast_select_fusion), channel_id=1, source_target_pairs={{0,64},{4,68},{1,17},{5,21},{2,66},{6,70},{3,19},{7,23}} | collective-permute-start | bytes 1179656 | tf_op jit(solution)/shard_map/ppermute | solution.py:416
  26.3 21.6 %collective-permute-start.6 = (bf16[4,2,64,384]{3,2,1,0:T(8,128)(2,1)S(1)}, bf16[4,2,64,384]{3,2,1,0:T(8,128)(2,1)S(1)}, u32[]{:S(2)}, u32[]{:S(2)}) collective-permute-start(bf16[4,2,64,384]{3,2,1,0:T(8,128)(2,1)S(1)} %broadcast_select_fusion.1), channel_id=1, source_target_pairs={{0,64},{4,68},{1,17},{5,21},{2,66},{6,70},{3,19},{7,23}} | collective-permute-start | bytes 1179656 | tf_op jit(solution)/shard_map/ppermute | solution.py:416
  27.1 21.6 %collective-permute-start.15 = (bf16[4,2,64,384]{3,2,1,0:T(8,128)(2,1)S(1)}, bf16[4,2,64,384]{3,2,1,0:T(8,128)(2,1)S(1)}, u32[]{:S(2)}, u32[]{:S(2)}) collective-permute-start(bf16[4,2,64,384]{3,2,1,0:T(8,128)(2,1)S(1)} %broadcast_select_fusion.2), channel_id=1, source_target_pairs={{0,96},{4,100},{64,32},{68,36},{1,25},{5,29},{17,9},{21,13},{2,98}... | collective-permute-start | bytes 1179656 | tf_op jit(solution)/shard_map/ppermute | solution.py:416
  34.1 51.0 %collective-permute-start.2 = (bf16[12,64,384]{2,1,0:T(8,128)(2,1)}, bf16[12,64,384]{2,1,0:T(8,128)(2,1)}, u32[]{:S(2)}, u32[]{:S(2)}) collective-permute-start(bf16[12,64,384]{2,1,0:T(8,128)(2,1)} %get-tuple-element.32.e3_ref), channel_id=1, source_target_pairs={{0,1},{1,2},{2,3},{4,5},{5,6},{6,7},{8,9},{9,10},{10,11},{12,13},{... | collective-permute-start | bytes 1769480 | tf_op jit(solution)/shard_map/ppermute | solution.py:327
  40.7 45.7 %collective-permute-start.3 = (bf16[12,64,384]{2,1,0:T(8,128)(2,1)}, bf16[12,64,384]{2,1,0:T(8,128)(2,1)}, u32[]{:S(2)}, u32[]{:S(2)}) collective-permute-start(bf16[12,64,384]{2,1,0:T(8,128)(2,1)} %get-tuple-element.33.e0_ref), channel_id=1, source_target_pairs={{1,0},{2,1},{3,2},{5,4},{6,5},{7,6},{9,8},{10,9},{11,10},{13,12},{... | collective-permute-start | bytes 1769480 | tf_op jit(solution)/shard_map/ppermute | solution.py:328
  48.0 13.8 %collective-permute-start.7 = (bf16[4,2,64,384]{3,2,1,0:T(8,128)(2,1)S(1)}, bf16[4,2,64,384]{3,2,1,0:T(8,128)(2,1)S(1)}, u32[]{:S(2)}, u32[]{:S(2)}) collective-permute-start(bf16[4,2,64,384]{3,2,1,0:T(8,128)(2,1)S(1)} %broadcast_select_fusion.3), channel_id=1, source_target_pairs={{0,96},{4,100},{64,32},{68,36},{1,25},{5,29},{17,9},{21,13},{2,98}... | collective-permute-start | bytes 1179656 | tf_op jit(solution)/shard_map/ppermute | solution.py:416
  48.8 13.7 %collective-permute-start.16 = (bf16[4,2,64,384]{3,2,1,0:T(8,128)(2,1)S(1)}, bf16[4,2,64,384]{3,2,1,0:T(8,128)(2,1)S(1)}, u32[]{:S(2)}, u32[]{:S(2)}) collective-permute-start(bf16[4,2,64,384]{3,2,1,0:T(8,128)(2,1)S(1)} %broadcast_select_fusion.4), channel_id=1, source_target_pairs={{0,24},{4,28},{64,88},{68,92},{96,120},{100,124},{32,56},{36,60},{... | collective-permute-start | bytes 1179656 | tf_op jit(solution)/shard_map/ppermute | solution.py:416
  49.5 11.5 %copy-start.2 = (bf16[384,384]{1,0:T(8,128)(2,1)S(1)}, bf16[384,384]{1,0:T(8,128)(2,1)}, u32[]{:S(2)}) copy-start(bf16[384,384]{1,0:T(8,128)(2,1)} %param.18) | copy-start | bytes 884740
  58.9 6.6 %copy-start.7 = (bf16[15,64,384]{2,1,0:T(8,128)(2,1)S(1)}, bf16[15,64,384]{2,1,0:T(8,128)(2,1)}, u32[]{:S(2)}) copy-start(bf16[15,64,384]{2,1,0:T(8,128)(2,1)} %get-tuple-element.45.own_ref) | copy-start | bytes 2211844
  58.9 46.4 %collective-permute-start.19 = (bf16[15,64,384]{2,1,0:T(8,128)(2,1)}, bf16[15,64,384]{2,1,0:T(8,128)(2,1)}, u32[]{:S(2)}, u32[]{:S(2)}) collective-permute-start(bf16[15,64,384]{2,1,0:T(8,128)(2,1)} %get-tuple-element.48.own_ref), channel_id=1, source_target_pairs={{0,4},{4,8},{8,12},{12,16},{16,20},{20,24},{24,28},{28,32},{32,36}... | collective-permute-start | bytes 2211848 | tf_op jit(solution)/shard_map/ppermute | solution.py:423
  61.8 3.7 %collective-permute-start.8 = (bf16[4,2,64,384]{3,2,1,0:T(8,128)(2,1)S(1)}, bf16[4,2,64,384]{3,2,1,0:T(8,128)(2,1)S(1)}, u32[]{:S(2)}, u32[]{:S(2)}) collective-permute-start(bf16[4,2,64,384]{3,2,1,0:T(8,128)(2,1)S(1)} %broadcast_select_fusion.5), channel_id=1, source_target_pairs={{0,24},{4,28},{64,88},{68,92},{96,120},{100,124},{32,56},{36,60},{... | collective-permute-start | bytes 1179656 | tf_op jit(solution)/shard_map/ppermute | solution.py:416
  62.6 21.1 %collective-permute-start.17 = (bf16[4,2,64,384]{3,2,1,0:T(8,128)(2,1)S(1)}, bf16[4,2,64,384]{3,2,1,0:T(8,128)(2,1)S(1)}, u32[]{:S(2)}, u32[]{:S(2)}) collective-permute-start(bf16[4,2,64,384]{3,2,1,0:T(8,128)(2,1)S(1)} %broadcast_select_fusion.6), channel_id=1, source_target_pairs={{24,16},{28,20},{88,80},{92,84},{120,112},{124,116},{56,48},{60,52... | collective-permute-start | bytes 1179656 | tf_op jit(solution)/shard_map/ppermute | solution.py:416
  65.5 51.3 %collective-permute-start.12 = (bf16[15,64,384]{2,1,0:T(8,128)(2,1)S(1)}, bf16[15,64,384]{2,1,0:T(8,128)(2,1)}, u32[]{:S(2)}, u32[]{:S(2)}) collective-permute-start(bf16[15,64,384]{2,1,0:T(8,128)(2,1)S(1)} %copy-done.7), channel_id=1, source_target_pairs={{0,4},{4,8},{8,12},{12,16},{16,20},{20,24},{24,28},{28,32},{32,36}... | collective-permute-start | bytes 2211848 | tf_op jit(solution)/shard_map/ppermute | solution.py:423
  83.7 11.7 %collective-permute-start.9 = (bf16[4,2,64,384]{3,2,1,0:T(8,128)(2,1)S(1)}, bf16[4,2,64,384]{3,2,1,0:T(8,128)(2,1)S(1)}, u32[]{:S(2)}, u32[]{:S(2)}) collective-permute-start(bf16[4,2,64,384]{3,2,1,0:T(8,128)(2,1)S(1)} %broadcast_select_fusion.7), channel_id=1, source_target_pairs={{24,16},{28,20},{88,80},{92,84},{120,112},{124,116},{56,48},{60,52... | collective-permute-start | bytes 1179656 | tf_op jit(solution)/shard_map/ppermute | solution.py:416
  85.1 17.3 %collective-permute-start.18 = (bf16[4,2,64,384]{3,2,1,0:T(8,128)(2,1)S(1)}, bf16[4,2,64,384]{3,2,1,0:T(8,128)(2,1)S(1)}, u32[]{:S(2)}, u32[]{:S(2)}) collective-permute-start(bf16[4,2,64,384]{3,2,1,0:T(8,128)(2,1)S(1)} %broadcast_select_fusion.8), channel_id=1, source_target_pairs={{16,8},{20,12},{80,72},{84,76},{112,104},{116,108},{48,40},{52,44}... | collective-permute-start | bytes 1179656 | tf_op jit(solution)/shard_map/ppermute | solution.py:416
  93.4 35.7 %collective-permute-start.11 = (bf16[15,64,384]{2,1,0:T(8,128)(2,1)}, bf16[15,64,384]{2,1,0:T(8,128)(2,1)}, u32[]{:S(2)}, u32[]{:S(2)}) collective-permute-start(bf16[15,64,384]{2,1,0:T(8,128)(2,1)} %get-tuple-element.43.own_ref), channel_id=1, source_target_pairs={{0,4},{4,8},{8,12},{12,16},{16,20},{20,24},{24,28},{28,32},{32,36}... | collective-permute-start | bytes 2211848 | tf_op jit(solution)/shard_map/ppermute | solution.py:423
  95.4 45.3 %collective-permute-start.4 = (bf16[15,64,384]{2,1,0:T(8,128)(2,1)}, bf16[15,64,384]{2,1,0:T(8,128)(2,1)S(1)}, u32[]{:S(2)}, u32[]{:S(2)}) collective-permute-start(bf16[15,64,384]{2,1,0:T(8,128)(2,1)} %get-tuple-element.40.own_ref), channel_id=1, source_target_pairs={{0,4},{4,8},{8,12},{12,16},{16,20},{20,24},{24,28},{28,32},{32,36}... | collective-permute-start | bytes 2211848 | tf_op jit(solution)/shard_map/ppermute | solution.py:423
  102.4 26.0 %collective-permute-start.10 = (bf16[4,2,64,384]{3,2,1,0:T(8,128)(2,1)S(1)}, bf16[4,2,64,384]{3,2,1,0:T(8,128)(2,1)S(1)}, u32[]{:S(2)}, u32[]{:S(2)}) collective-permute-start(bf16[4,2,64,384]{3,2,1,0:T(8,128)(2,1)S(1)} %broadcast_select_fusion.9), channel_id=1, source_target_pairs={{16,8},{20,12},{80,72},{84,76},{112,104},{116,108},{48,40},{52,44}... | collective-permute-start | bytes 1179656 | tf_op jit(solution)/shard_map/ppermute | solution.py:416
  (7 other events, 20.8 us)
where the time goes:
time: 154 us; the launch traced here: 153 us
  Pallas kernels  79.5 us (52%)
  starting transfers between devices  60 us (39%)
  local copies, waits for them, and re-layouts  5.2 us (3%)
  waiting for transfers between devices  3.2 us (2%)
  other arithmetic  3.2 us (2%)
    pallas_call x4, Pallas kernels, on_device(): pl.pallas_call(attend_kernel, grid_spec=pltpu.PrefetchScalarGridSpec(num_...  46 us
    ppermute x4, starting transfers between devices, on_device(): halos[r] = lax.ppermute(wins[r], 'tm', shift)  29 us
    pallas_call x2, Pallas kernels, on_device(): pl.pallas_call(functools.partial(inner_kernel, f0, n), grid=(n // step,),...  14 us
    ppermute x12, starting transfers between devices, on_device(): got = lax.ppermute(held[tree], ('tm', 'space'), pairs)  11.6 us
    ppermute x2, starting transfers between devices, on_device(): down = lax.ppermute(e0, 'space', down_pairs)  10.8 us
    pallas_call x2, Pallas kernels, on_device(): pl.pallas_call(functools.partial(edge_kernel, f0, n_sp - 1), grid_spec=pl...  10.1 us
    pallas_call x2, Pallas kernels, on_device(): pl.pallas_call(functools.partial(embed_kernel, f0, n, (0, R - 1)), grid=(...  9.37 us
    ppermute x2, starting transfers between devices, on_device(): up = lax.ppermute(e3, 'space', up_pairs)  8.58 us
  transfers between devices with their start and end apart: 20, of which 2 were waited for; matrix products, arithmetic and copies ran while one was open for 4% of the time, Pallas kernels for 39%

commit v1 on v0

--- a/solution.py
+++ b/solution.py
@@ -7,7 +7,6 @@
 from jax.experimental.pallas import tpu as pltpu
 from jax.sharding import PartitionSpec as P
 
-ACTIONS = 8
 WINDOW = 16
 ANCHORS = 4
 BF = jnp.bfloat16
@@ -54,7 +53,8 @@
 
 
 def embed_kernel(
-    frame0, count, pair, ids_ref, act_ref, table_ref, top_ref, low_ref, a_ref, b_ref, hi, lo
+    frame0, count, pair, action_ref, ids_ref, act_ref, table_ref, top_ref, low_ref, a_ref, b_ref,
+    hi, lo,
 ):
     f = pl.program_id(0)
 
@@ -65,8 +65,11 @@
     step = top_ref.shape[0]
     at = pl.ds(pl.multiple_of(128 * step * f, 128), 128 * step)
     token = lookup(hi[at, :], lo[at, :], table_ref)
+    actions = act_ref[...].astype(F32)
+    index = lax.broadcasted_iota(jnp.int32, actions.shape, 0)
     for i in range(step):
-        act = act_ref[pl.ds(frame0 + step * f + i, 1), :]
+        picked = index == action_ref[frame0 + step * f + i]
+        act = jnp.sum(jnp.where(picked, actions, F32(0)), axis=0, keepdims=True)
         for k, ref, to in ((0, top_ref, a_ref), (1, low_ref, b_ref)):
             t = token[128 * i + 64 * k : 128 * i + 64 * k + 64]
             to[i] = (ref[i, 0].astype(F32) + t + act).astype(BF)
@@ -102,8 +105,8 @@
 
 
 def inner_kernel(
-    frame0, count, ids_ref, act_ref, table_ref, top_ref, low_ref, e0_ref, e3_ref, cw_ref, gain_ref,
-    *rest
+    frame0, count, action_ref, ids_ref, act_ref, table_ref, top_ref, low_ref, e0_ref, e3_ref, cw_ref,
+    gain_ref, *rest
 ):
     held = rest[:2] if frame0 else ()
     rest = rest[len(held) :]
@@ -111,7 +114,8 @@
     anc_ref = None if frame0 else rest[5]
     hi, lo = rest[-2:]
     embed_kernel(
-        frame0, count, (1, 2), ids_ref, act_ref, table_ref, top_ref, low_ref, e1_ref, e2_ref, hi, lo
+        frame0, count, (1, 2), action_ref, ids_ref, act_ref, table_ref, top_ref, low_ref, e1_ref,
+        e2_ref, hi, lo,
     )
     rows = (e0_ref, e1_ref, e2_ref, e3_ref)
 
@@ -145,8 +149,8 @@
 
 
 def attend_kernel(
-    first_ref, own0_ref, own_ref, halo_ref, anc_ref, mix_a_ref, mix_b_ref, wqkv_ref,
-    wo_ref, *rest
+    first_ref, own0_ref, own_ref, halo_ref, anc_ref, mix_a_ref, mix_b_ref, mix_c_ref, wq_ref,
+    wk_ref, wv_ref, wo_ref, *rest
 ):
     out_ref, qs, ks, vs, hk, hv, ak, av, att, bias = rest[-10:]
     D = 384
@@ -161,10 +165,9 @@
                 to[j, pl.ds(row0 + i * gap, every), :] = piece
 
     def qkv(x, row0, q_to, k_to, v_to):
-        for i, to in enumerate((q_to, k_to, v_to)):
+        for w_ref, to in ((wq_ref, q_to), (wk_ref, k_to), (wv_ref, v_to)):
             if to is not None:
-                w = wqkv_ref[:, D * i : D * i + D]
-                put(to, row0, jnp.dot(x, w, preferred_element_type=F32))
+                put(to, row0, jnp.dot(x, w_ref[...], preferred_element_type=F32))
 
     qkv(own0_ref[0, 0], 0, qs, ks, vs)
     zero = jnp.zeros((cols, D), F32)
@@ -206,7 +209,7 @@
     low = lane < 64
     c = F32(LOG2E / 8.0)
 
-    GROUPS = 4
+    GROUPS = 8
 
     @pl.loop(0, cols // (4 * GROUPS))
     def _(g):
@@ -262,7 +265,7 @@
         put(qs, i * 16 * 17, jnp.dot(x, wo_ref[...], preferred_element_type=F32), 16, 17)
 
     t0 = 0
-    for mixed_ref in (mix_a_ref, mix_b_ref):
+    for mixed_ref in (mix_a_ref, mix_b_ref, mix_c_ref):
 
         @pl.loop(0, mixed_ref.shape[0])
         def _(i, t0=t0, mixed_ref=mixed_ref):
@@ -287,22 +290,28 @@
     F, R, C, D = frames.shape
     tm, sp = lax.axis_index("tm"), lax.axis_index("space")
     n_tm, n_sp = lax.axis_size("tm"), lax.axis_size("space")
-    onehot = (action_ids[:, None] == jnp.arange(ACTIONS, dtype=jnp.int32)[None, :]).astype(BF)
-    act = jnp.dot(onehot, action_table, preferred_element_type=F32)
     cw, gain = conv_weight, norm_gain.reshape(1, D)
-    wqkv = jnp.concatenate([w_query, w_key, w_value], axis=1)
 
     up_pairs = [(i, i + 1) for i in range(n_sp - 1)]
     down_pairs = [(j, i) for i, j in up_pairs]
     step = 2
-    parts = ((0, 4), (4, 12))
-    table_specs = [whole((1, F, R, C)), whole((F, D)), whole(token_table.shape)]
+    early = ((0, 4), (4, 12))
+    parts = ((0, 4), (4, 6), (10, 6))
+    table_specs = [
+        pl.BlockSpec(memory_space=pltpu.SMEM),
+        whole((1, F, R, C)),
+        whole(action_table.shape),
+        whole(token_table.shape),
+    ]
     conv_specs = [whole((3, 3, D)), whole((1, D))]
 
     def row_of(r, f0=0):
         return pl.BlockSpec((step, 1, C, D), lambda f, *_: (f0 // step + f, r, 0, 0))
 
-    line = pl.BlockSpec((step, C, D), lambda f, *_: (f, 0, 0))
+    def line_of(f0=0):
+        return pl.BlockSpec((step, C, D), lambda f, *_: (f0 // step + f, 0, 0))
+
+    line = line_of()
     pair = pl.BlockSpec((step, 2, C, D), lambda f, *_: (f, 0, 0, 0))
 
     def shape(n, *k):
@@ -313,7 +322,7 @@
 
     flags = sp.astype(jnp.int32).reshape(1)
     edges = []
-    for (f0, n) in parts:
+    for (f0, n) in early:
         e0, e3 = pl.pallas_call(
             functools.partial(embed_kernel, f0, n, (0, R - 1)),
             grid=(n // step,),
@@ -323,7 +332,7 @@
             scratch_shapes=[pltpu.VMEM((n * 2 * C, 128), BF)] * 2,
             cost_estimate=cost(n / 2),
             name="embed",
-        )(token_ids, act, token_table, frames, frames)
+        )(action_ids, token_ids, action_table, token_table, frames, frames)
         up = lax.ppermute(e3, "space", up_pairs)
         down = lax.ppermute(e0, "space", down_pairs)
         edges.append((e0, e3, up, down))
@@ -338,8 +347,9 @@
     inner, mids, mixed12 = [], [], []
     for p, (f0, n) in enumerate(parts):
         shapes, specs = win_outs(f0, n)
-        in_specs = table_specs + [row_of(1, f0), row_of(2, f0), line, line] + conv_specs
-        operands = [token_ids, act, token_table, frames, frames, *edges[p][:2], cw, gain]
+        in_specs = table_specs + [row_of(1, f0), row_of(2, f0)] + [line_of(f0 - early[min(p, 1)][0])] * 2 + conv_specs
+        operands = [action_ids, token_ids, action_table, token_table, frames, frames]
+        operands += [*edges[min(p, 1)][:2], cw, gain]
         if f0:
             in_specs += [whole((f0 - 1, C, D))] * 2
             operands += inner[-1][:2]
@@ -363,8 +373,9 @@
     outer, mixed03 = [], []
     for p, (f0, n) in enumerate(parts):
         shapes, specs = win_outs(f0, n)
-        e0, e3, up, down = edges[p]
-        in_specs = [line] * 6 + conv_specs
+        e0, e3, up, down = edges[min(p, 1)]
+        far = line_of(f0 - early[min(p, 1)][0])
+        in_specs = [far, far, line, line, far, far] + conv_specs
         operands = [flags, up, e0, *mids[p], e3, down, cw, gain]
         if f0:
             in_specs += [whole((f0 - 1, C, D))] * 2
@@ -439,9 +450,10 @@
         in_specs += [
             pl.BlockSpec((n, 1, C, D), lambda i, *_, k=k: (0, k, 0, 0), **one) for _, n in parts
         ]
-        in_specs += [whole((D, 3 * D)), whole((D, D))]
+        in_specs += [whole((D, D))] * 4
         operands = [
-            first, own_anchors[tree], wins[r], halos[r], held[tree], *mixed, wqkv, w_out
+            first, own_anchors[tree], wins[r], halos[r], held[tree], *mixed, w_query,
+            w_key, w_value, w_out,
         ]
         aliases = {}
         if out is not None:

time: 154 us -> 146 us (0.948)
  the two profiles are of different devices: /device:TPU:22 before, /device:TPU:50 now
where the time goes in v1:
time: 146 us; the launch traced here: 144 us
  Pallas kernels  83.6 us (57%)
  starting transfers between devices  39.7 us (27%)
  waiting for transfers between devices  14.8 us (10%)
  local copies, waits for them, and re-layouts  3.7 us (3%)
  other arithmetic  2.11 us (1%)
    pallas_call x4, Pallas kernels, on_device(): pl.pallas_call(attend_kernel, grid_spec=pltpu.PrefetchScalarGridSpec(num_...  45 us
    ppermute x4, starting transfers between devices, on_device(): halos[r] = lax.ppermute(wins[r], 'tm', shift)  17.4 us
    pallas_call x3, Pallas kernels, on_device(): pl.pallas_call(functools.partial(inner_kernel, f0, n), grid=(n // step,),...  16.6 us
    pallas_call x3, Pallas kernels, on_device(): pl.pallas_call(functools.partial(edge_kernel, f0, n_sp - 1), grid_spec=pl...  12.6 us
    ppermute x12, waiting for transfers between devices, on_device(): got = lax.ppermute(held[tree], ('tm', 'space'), pairs)  11.6 us
    ppermute x12, starting transfers between devices, on_device(): got = lax.ppermute(held[tree], ('tm', 'space'), pairs)  11 us
    pallas_call x2, Pallas kernels, on_device(): pl.pallas_call(functools.partial(embed_kernel, f0, n, (0, R - 1)), grid=(...  9.39 us
    ppermute x2, starting transfers between devices, on_device(): down = lax.ppermute(e0, 'space', down_pairs)  7.46 us
  transfers between devices with their start and end apart: 20, of which 4 were waited for; matrix products, arithmetic and copies ran while one was open for 1% of the time, Pallas kernels for 45%

profile of v1, /device:TPU:50, one launch (start us, length us, event | category | flops | bytes accessed | tf_op | source)
XLA Modules:
  0.0 144.4 jit_solution(6068380746878278271)
XLA Ops:
  1.3 3.1 %embed.2 = (bf16[4,64,384]{2,1,0:T(8,128)(2,1)}, bf16[4,64,384]{2,1,0:T(8,128)(2,1)}) custom-call(s32[16]{0:T(128)} %action_ref.9, s32[1,16,4,64]{3,2,1,0:T(4,128)} %ids_ref.9, bf16[8,384]{1,0:T(8,128)(2,1)} %act_ref.9, bf16[1024,384]{1,0:T(8,128)(2,1)} %table_ref.9, bf16[16,4,64,384]{3,2,1,0:T(8,128)(2,1)} %low_ref.9, bf16[16,4,64,384]{3,2,1,0:T(8,128)(2,1)} %low_ref.9), custom_call_target="tpu_custom_call" | custom-call | flops 800000000 | bytes 200000 | tf_op jit(solution)/shard_map/embed/pallas_call | solution.py:326
  4.3 4.5 %inner.3 = (bf16[4,64,384]{2,1,0:T(8,128)(2,1)}, bf16[4,64,384]{2,1,0:T(8,128)(2,1)}, bf16[3,64,384]{2,1,0:T(8,128)(2,1)}, bf16[3,64,384]{2,1,0:T(8,128)(2,1)}, ...) custom-call(s32[16]{0:T(128)} %action_ref.9, s32[1,16,4,64]{3,2,1,0:T(4,128)} %ids_ref.9, ...), custom_call_target="tpu_custom_call" | custom-call | flops 1600000000 | bytes 400000 | tf_op jit(solution)/shard_map/inner/pallas_call | solution.py:359
  9.7 1.9 %collective-permute-start = (bf16[4,64,384]{2,1,0:T(8,128)(2,1)S(1)}, bf16[4,64,384]{2,1,0:T(8,128)(2,1)S(1)}, u32[]{:S(2)}, u32[]{:S(2)}) collective-permute-start(bf16[4,64,384]{2,1,0:T(8,128)(2,1)S(1)} %copy-done.3), channel_id=1, source_target_pairs={{0,1},{1,2},{2,3},{4,5},{5,6},{6,7},{8,9},{9,10},{10,11},{12,13},{... | collective-permute-start | bytes 589832 | tf_op jit(solution)/shard_map/ppermute | solution.py:336
  11.6 3.6 %collective-permute-start.1 = (bf16[4,64,384]{2,1,0:T(8,128)(2,1)S(1)}, bf16[4,64,384]{2,1,0:T(8,128)(2,1)S(1)}, u32[]{:S(2)}, u32[]{:S(2)}) collective-permute-start(bf16[4,64,384]{2,1,0:T(8,128)(2,1)S(1)} %copy-done.2), channel_id=1, source_target_pairs={{1,0},{2,1},{3,2},{5,4},{6,5},{7,6},{9,8},{10,9},{11,10},{13,12},{... | collective-permute-start | bytes 589832 | tf_op jit(solution)/shard_map/ppermute | solution.py:337
  15.3 1.4 collective-permute-done.up_ref
  16.7 1.8 %collective-permute-done.1.down_ref = bf16[4,64,384]{2,1,0:T(8,128)(2,1)S(1)} collective-permute-done((bf16[4,64,384]{2,1,0:T(8,128)(2,1)S(1)}, bf16[4,64,384]{2,1,0:T(8,128)(2,1)S(1)}, u32[]{:S(2)}, u32[]{:S(2)}) %collective-permute-start.1) | collective-permute-done | bytes 196640 | tf_op jit(solution)/shard_map/ppermute | solution.py:337
  19.1 3.1 %edge.3 = (bf16[3,64,384]{2,1,0:T(8,128)(2,1)}, bf16[3,64,384]{2,1,0:T(8,128)(2,1)}, f32[4,2,64,384]{3,2,1,0:T(8,128)}, bf16[4,2,64,384]{3,2,1,0:T(8,128)(2,1)}) custom-call(s32[1]{0:T(128)} %bitcast.1.flag_ref, bf16[4,64,384]{2,1,0:T(8,128)(2,1)} %copy-done.6, bf16[4,64,384]{2,1,0:T(8,128)(2,1)} %get-tuple-element.36.e0_ref, ...), custom_call_target="tpu_custom_call" | custom-call | flops 1600000000 | bytes 400000 | tf_op jit(solution)/shard_map/edge/pallas_call | solution.py:386
  23.8 6.3 %embed.3 = (bf16[12,64,384]{2,1,0:T(8,128)(2,1)}, bf16[12,64,384]{2,1,0:T(8,128)(2,1)}) custom-call(s32[16]{0:T(128)} %action_ref.9, s32[1,16,4,64]{3,2,1,0:T(4,128)} %ids_ref.9, bf16[8,384]{1,0:T(8,128)(2,1)} %act_ref.9, bf16[1024,384]{1,0:T(8,128)(2,1)} %table_ref.9, bf16[16,4,64,384]{3,2,1,0:T(8,128)(2,1)} %low_ref.9, bf16[16,4,64,384]{3,2,1,0:T(8,128)(2,1)} %low_ref.9), custom_call_target="tpu_custom_call" | custom-call | flops 2400000000 | bytes 600000 | tf_op jit(solution)/shard_map/embed/pallas_call | solution.py:326
  30.2 1.9 %collective-permute-start.2 = (bf16[12,64,384]{2,1,0:T(8,128)(2,1)}, bf16[12,64,384]{2,1,0:T(8,128)(2,1)}, u32[]{:S(2)}, u32[]{:S(2)}) collective-permute-start(bf16[12,64,384]{2,1,0:T(8,128)(2,1)} %get-tuple-element.40.e3_ref), channel_id=1, source_target_pairs={{0,1},{1,2},{2,3},{4,5},{5,6},{6,7},{8,9},{9,10},{10,11},{12,13},{... | collective-permute-start | bytes 1769480 | tf_op jit(solution)/shard_map/ppermute | solution.py:336
  32.1 3.8 %collective-permute-start.3 = (bf16[12,64,384]{2,1,0:T(8,128)(2,1)}, bf16[12,64,384]{2,1,0:T(8,128)(2,1)}, u32[]{:S(2)}, u32[]{:S(2)}) collective-permute-start(bf16[12,64,384]{2,1,0:T(8,128)(2,1)} %get-tuple-element.41.e0_ref), channel_id=1, source_target_pairs={{1,0},{2,1},{3,2},{5,4},{6,5},{7,6},{9,8},{10,9},{11,10},{13,12},{... | collective-permute-start | bytes 1769480 | tf_op jit(solution)/shard_map/ppermute | solution.py:337
  37.5 5.8 %inner.4 = (bf16[6,64,384]{2,1,0:T(8,128)(2,1)}, bf16[6,64,384]{2,1,0:T(8,128)(2,1)}, bf16[9,64,384]{2,1,0:T(8,128)(2,1)}, bf16[9,64,384]{2,1,0:T(8,128)(2,1)}, f32[6,2,64,384]{3,2,1,0:T(8,128)}) custom-call(s32[16]{0:T(128)} %action_ref.9, s32[1,16,4,64]{3,2,1,0:T(4,128)} %ids_ref.9, bf16[8,384]{1,0:T(8,128)(2,1)} %act_ref.9, bf16[1024,384]{1,0:T(8,128)(2,1)} %table_ref.9, ...), custom_call_target="tpu_custom_call" | custom-call | flops 2400000000 | bytes 600000 | tf_op jit(solution)/shard_map/inner/pallas_call | solution.py:359
  44.8 6.3 %inner.5 = (bf16[6,64,384]{2,1,0:T(8,128)(2,1)}, bf16[6,64,384]{2,1,0:T(8,128)(2,1)}, bf16[15,64,384]{2,1,0:T(8,128)(2,1)}, bf16[15,64,384]{2,1,0:T(8,128)(2,1)}, f32[6,2,64,384]{3,2,1,0:T(8,128)}) custom-call(s32[16]{0:T(128)} %action_ref.9, s32[1,16,4,64]{3,2,1,0:T(4,128)} %ids_ref.9, bf16[8,384]{1,0:T(8,128)(2,1)} %act_ref.9, ...), custom_call_target="tpu_custom_call" | custom-call | flops 2400000000 | bytes 600000 | tf_op jit(solution)/shard_map/inner/pallas_call | solution.py:359
  51.2 4.0 %collective-permute-start.19 = (bf16[15,64,384]{2,1,0:T(8,128)(2,1)}, bf16[15,64,384]{2,1,0:T(8,128)(2,1)S(1)}, u32[]{:S(2)}, u32[]{:S(2)}) collective-permute-start(bf16[15,64,384]{2,1,0:T(8,128)(2,1)} %get-tuple-element.64.own_ref), channel_id=1, source_target_pairs={{0,4},{4,8},{8,12},{12,16},{16,20},{20,24},{24,28},{28,32},{32,36}... | collective-permute-start | bytes 2211848 | tf_op jit(solution)/shard_map/ppermute | solution.py:434
  55.2 4.6 %collective-permute-start.12 = (bf16[15,64,384]{2,1,0:T(8,128)(2,1)}, bf16[15,64,384]{2,1,0:T(8,128)(2,1)}, u32[]{:S(2)}, u32[]{:S(2)}) collective-permute-start(bf16[15,64,384]{2,1,0:T(8,128)(2,1)} %get-tuple-element.60.own_ref), channel_id=1, source_target_pairs={{0,4},{4,8},{8,12},{12,16},{16,20},{20,24},{24,28},{28,32},{32,36}... | collective-permute-start | bytes 2211848 | tf_op jit(solution)/shard_map/ppermute | solution.py:434
  62.0 4.6 %edge.4 = (bf16[9,64,384]{2,1,0:T(8,128)(2,1)}, bf16[9,64,384]{2,1,0:T(8,128)(2,1)}, f32[6,2,64,384]{3,2,1,0:T(8,128)}) custom-call(s32[1]{0:T(128)} %bitcast.1.flag_ref, bf16[12,64,384]{2,1,0:T(8,128)(2,1)} %collective-permute-done.2.up_ref, bf16[12,64,384]{2,1,0:T(8,128)(2,1)} %get-tuple-element.41.e0_ref, bf16[6,64,384]{2,1,0:T(8,128)(2,1)} %get-tuple-element.48.e1_ref, ...), custom_call_target="tpu_custom_call" | custom-call | flops 2400000000 | bytes 600000 | tf_op jit(solution)/shard_map/edge/pallas_call | solution.py:386
  68.0 10.3 %collective-permute-done.17 = bf16[4,2,64,384]{3,2,1,0:T(8,128)(2,1)S(1)} collective-permute-done((bf16[4,2,64,384]{3,2,1,0:T(8,128)(2,1)S(1)}, bf16[4,2,64,384]{3,2,1,0:T(8,128)(2,1)S(1)}, u32[]{:S(2)}, u32[]{:S(2)}) %collective-permute-start.17) | collective-permute-done | bytes 393248 | tf_op jit(solution)/shard_map/ppermute | solution.py:427
  79.6 5.0 %edge.5 = (bf16[15,64,384]{2,1,0:T(8,128)(2,1)}, bf16[15,64,384]{2,1,0:T(8,128)(2,1)}, f32[6,2,64,384]{3,2,1,0:T(8,128)}) custom-call(s32[1]{0:T(128)} %bitcast.1.flag_ref, bf16[12,64,384]{2,1,0:T(8,128)(2,1)} %collective-permute-done.2.up_ref, bf16[12,64,384]{2,1,0:T(8,128)(2,1)} %get-tuple-element.41.e0_ref, bf16[6,64,384]{2,1,0:T(8,128)(2,1)} %get-tuple-element.46.e1_ref, ...), custom_call_target="tpu_custom_call" | custom-call | flops 2400000000 | bytes 600000 | tf_op jit(solution)/shard_map/edge/pallas_call | solution.py:386
  84.6 1.9 %collective-permute-start.11 = (bf16[15,64,384]{2,1,0:T(8,128)(2,1)}, bf16[15,64,384]{2,1,0:T(8,128)(2,1)}, u32[]{:S(2)}, u32[]{:S(2)}) collective-permute-start(bf16[15,64,384]{2,1,0:T(8,128)(2,1)} %get-tuple-element.58.own_ref), channel_id=1, source_target_pairs={{0,4},{4,8},{8,12},{12,16},{16,20},{20,24},{24,28},{28,32},{32,36}... | collective-permute-start | bytes 2211848 | tf_op jit(solution)/shard_map/ppermute | solution.py:434
  87.8 6.8 %collective-permute-start.4 = (bf16[15,64,384]{2,1,0:T(8,128)(2,1)}, bf16[15,64,384]{2,1,0:T(8,128)(2,1)S(1)}, u32[]{:S(2)}, u32[]{:S(2)}) collective-permute-start(bf16[15,64,384]{2,1,0:T(8,128)(2,1)} %get-tuple-element.54.own_ref), channel_id=1, source_target_pairs={{0,4},{4,8},{8,12},{12,16},{16,20},{20,24},{24,28},{28,32},{32,36}... | collective-permute-start | bytes 2211848 | tf_op jit(solution)/shard_map/ppermute | solution.py:434
  94.7 1.3 collective-permute-start.10
  97.7 11.4 %attend.4.rest_0_ = bf16[16,4,64,384]{3,2,1,0:T(8,128)(2,1)} custom-call(s32[1]{0:T(128)} %bitcast.first_ref, bf16[4,2,64,384]{3,2,1,0:T(8,128)(2,1)} %get-tuple-element.59.own0_ref, bf16[15,64,384]{2,1,0:T(8,128)(2,1)} %get-tuple-element.64.own_ref, bf16[15,64,384]{2,1,0:T(8,128)(2,1)} %copy-done.4, ...), custom_call_target="tpu_custom_call" | custom-call | flops 4000000000 | bytes 1000000 | tf_op jit(solution)/shard_map/attend/pallas_call | solution.py:463
  109.1 11.2 %attend.5.rest_0_ = bf16[16,4,64,384]{3,2,1,0:T(8,128)(2,1)} custom-call(s32[1]{0:T(128)} %bitcast.first_ref, bf16[4,2,64,384]{3,2,1,0:T(8,128)(2,1)} %get-tuple-element.59.own0_ref, bf16[15,64,384]{2,1,0:T(8,128)(2,1)} %get-tuple-element.60.own_ref, bf16[15,64,384]{2,1,0:T(8,128)(2,1)} %collective-permute-done.12.halo_ref, ...), custom_call_target="tpu_custom_call", output_to_operand_aliasing={{}: (12, {})} | custom-call | flops 4000000000 | bytes 1000000 | tf_op jit(solution)/shard_map/attend/pallas_call | solution.py:463
  121.1 11.2 %attend.6.rest_0_ = bf16[16,4,64,384]{3,2,1,0:T(8,128)(2,1)} custom-call(s32[1]{0:T(128)} %bitcast.first_ref, bf16[4,2,64,384]{3,2,1,0:T(8,128)(2,1)} %get-tuple-element.39.own0_ref, bf16[15,64,384]{2,1,0:T(8,128)(2,1)} %get-tuple-element.58.own_ref, bf16[15,64,384]{2,1,0:T(8,128)(2,1)} %collective-permute-done.11.halo_ref, ...), custom_call_target="tpu_custom_call", output_to_operand_aliasing={{}: (12, {})} | custom-call | flops 4000000000 | bytes 1000000 | tf_op jit(solution)/shard_map/attend/pallas_call | solution.py:463
  133.2 11.2 %attend.7 = bf16[16,4,64,384]{3,2,1,0:T(8,128)(2,1)} custom-call(s32[1]{0:T(128)} %bitcast.first_ref, bf16[4,2,64,384]{3,2,1,0:T(8,128)(2,1)} %get-tuple-element.39.own0_ref, bf16[15,64,384]{2,1,0:T(8,128)(2,1)} %get-tuple-element.54.own_ref, bf16[15,64,384]{2,1,0:T(8,128)(2,1)} %copy-done.5, ...), custom_call_target="tpu_custom_call", output_to_operand_aliasing={{}: (12, {})} | custom-call | flops 4000000000 | bytes 1000000 | tf_op jit(solution)/shard_map/attend/pallas_call | solution.py:463
  (57 shorter events, 16.8 us)
Async XLA Ops:
  4.3 5.3 %copy-start.3 = (bf16[4,64,384]{2,1,0:T(8,128)(2,1)S(1)}, bf16[4,64,384]{2,1,0:T(8,128)(2,1)}, u32[]{:S(2)}) copy-start(bf16[4,64,384]{2,1,0:T(8,128)(2,1)} %get-tuple-element.35.e3_ref) | copy-start | bytes 589828
  4.3 7.3 %copy-start.2 = (bf16[4,64,384]{2,1,0:T(8,128)(2,1)S(1)}, bf16[4,64,384]{2,1,0:T(8,128)(2,1)}, u32[]{:S(2)}) copy-start(bf16[4,64,384]{2,1,0:T(8,128)(2,1)} %get-tuple-element.36.e0_ref) | copy-start | bytes 589828
  8.8 14.1 %copy-start = (bf16[4,2,64,384]{3,2,1,0:T(8,128)(2,1)S(1)}, bf16[4,2,64,384]{3,2,1,0:T(8,128)(2,1)}, u32[]{:S(2)}) copy-start(bf16[4,2,64,384]{3,2,1,0:T(8,128)(2,1)} %get-tuple-element.59.own0_ref) | copy-start | bytes 1179652
  8.9 14.1 %collective-permute-start.13 = (bf16[4,2,64,384]{3,2,1,0:T(8,128)(2,1)}, bf16[4,2,64,384]{3,2,1,0:T(8,128)(2,1)S(1)}, u32[]{:S(2)}, u32[]{:S(2)}) collective-permute-start(bf16[4,2,64,384]{3,2,1,0:T(8,128)(2,1)} %get-tuple-element.59.own0_ref), channel_id=1, source_target_pairs={{0,4},{1,5},{2,6},{3,7}} | collective-permute-start | bytes 1179656 | tf_op jit(solution)/shard_map/ppermute | solution.py:427
  9.7 7.0 %collective-permute-start = (bf16[4,64,384]{2,1,0:T(8,128)(2,1)S(1)}, bf16[4,64,384]{2,1,0:T(8,128)(2,1)S(1)}, u32[]{:S(2)}, u32[]{:S(2)}) collective-permute-start(bf16[4,64,384]{2,1,0:T(8,128)(2,1)S(1)} %copy-done.3), channel_id=1, source_target_pairs={{0,1},{1,2},{2,3},{4,5},{5,6},{6,7},{8,9},{9,10},{10,11},{12,13},{... | collective-permute-start | bytes 589832 | tf_op jit(solution)/shard_map/ppermute | solution.py:336
  11.6 6.8 %collective-permute-start.1 = (bf16[4,64,384]{2,1,0:T(8,128)(2,1)S(1)}, bf16[4,64,384]{2,1,0:T(8,128)(2,1)S(1)}, u32[]{:S(2)}, u32[]{:S(2)}) collective-permute-start(bf16[4,64,384]{2,1,0:T(8,128)(2,1)S(1)} %copy-done.2), channel_id=1, source_target_pairs={{1,0},{2,1},{3,2},{5,4},{6,5},{7,6},{9,8},{10,9},{11,10},{13,12},{... | collective-permute-start | bytes 589832 | tf_op jit(solution)/shard_map/ppermute | solution.py:337
  22.2 13.8 %collective-permute-start.5 = (bf16[4,2,64,384]{3,2,1,0:T(8,128)(2,1)}, bf16[4,2,64,384]{3,2,1,0:T(8,128)(2,1)S(1)}, u32[]{:S(2)}, u32[]{:S(2)}) collective-permute-start(bf16[4,2,64,384]{3,2,1,0:T(8,128)(2,1)} %get-tuple-element.39.own0_ref), channel_id=1, source_target_pairs={{0,4},{1,5},{2,6},{3,7}} | collective-permute-start | bytes 1179656 | tf_op jit(solution)/shard_map/ppermute | solution.py:427
  23.0 13.0 %copy-start.1 = (bf16[4,2,64,384]{3,2,1,0:T(8,128)(2,1)S(1)}, bf16[4,2,64,384]{3,2,1,0:T(8,128)(2,1)}, u32[]{:S(2)}) copy-start(bf16[4,2,64,384]{3,2,1,0:T(8,128)(2,1)} %get-tuple-element.39.own0_ref) | copy-start | bytes 1179652
  23.0 13.7 %collective-permute-start.14 = (bf16[4,2,64,384]{3,2,1,0:T(8,128)(2,1)S(1)}, bf16[4,2,64,384]{3,2,1,0:T(8,128)(2,1)S(1)}, u32[]{:S(2)}, u32[]{:S(2)}) collective-permute-start(bf16[4,2,64,384]{3,2,1,0:T(8,128)(2,1)S(1)} %broadcast_select_fusion), channel_id=1, source_target_pairs={{0,64},{4,68},{1,17},{5,21},{2,66},{6,70},{3,19},{7,23}} | collective-permute-start | bytes 1179656 | tf_op jit(solution)/shard_map/ppermute | solution.py:427
  30.2 30.5 %collective-permute-start.2 = (bf16[12,64,384]{2,1,0:T(8,128)(2,1)}, bf16[12,64,384]{2,1,0:T(8,128)(2,1)}, u32[]{:S(2)}, u32[]{:S(2)}) collective-permute-start(bf16[12,64,384]{2,1,0:T(8,128)(2,1)} %get-tuple-element.40.e3_ref), channel_id=1, source_target_pairs={{0,1},{1,2},{2,3},{4,5},{5,6},{6,7},{8,9},{9,10},{10,11},{12,13},{... | collective-permute-start | bytes 1769480 | tf_op jit(solution)/shard_map/ppermute | solution.py:336
  32.1 29.9 %collective-permute-start.3 = (bf16[12,64,384]{2,1,0:T(8,128)(2,1)}, bf16[12,64,384]{2,1,0:T(8,128)(2,1)}, u32[]{:S(2)}, u32[]{:S(2)}) collective-permute-start(bf16[12,64,384]{2,1,0:T(8,128)(2,1)} %get-tuple-element.41.e0_ref), channel_id=1, source_target_pairs={{1,0},{2,1},{3,2},{5,4},{6,5},{7,6},{9,8},{10,9},{11,10},{13,12},{... | collective-permute-start | bytes 1769480 | tf_op jit(solution)/shard_map/ppermute | solution.py:337
  36.0 7.3 %collective-permute-start.6 = (bf16[4,2,64,384]{3,2,1,0:T(8,128)(2,1)S(1)}, bf16[4,2,64,384]{3,2,1,0:T(8,128)(2,1)S(1)}, u32[]{:S(2)}, u32[]{:S(2)}) collective-permute-start(bf16[4,2,64,384]{3,2,1,0:T(8,128)(2,1)S(1)} %broadcast_select_fusion.1), channel_id=1, source_target_pairs={{0,64},{4,68},{1,17},{5,21},{2,66},{6,70},{3,19},{7,23}} | collective-permute-start | bytes 1179656 | tf_op jit(solution)/shard_map/ppermute | solution.py:427
  36.8 7.3 %collective-permute-start.15 = (bf16[4,2,64,384]{3,2,1,0:T(8,128)(2,1)S(1)}, bf16[4,2,64,384]{3,2,1,0:T(8,128)(2,1)S(1)}, u32[]{:S(2)}, u32[]{:S(2)}) collective-permute-start(bf16[4,2,64,384]{3,2,1,0:T(8,128)(2,1)S(1)} %broadcast_select_fusion.2), channel_id=1, source_target_pairs={{0,96},{4,100},{64,32},{68,36},{1,25},{5,29},{17,9},{21,13},{2,98}... | collective-permute-start | bytes 1179656 | tf_op jit(solution)/shard_map/ppermute | solution.py:427
  43.4 11.8 %collective-permute-start.7 = (bf16[4,2,64,384]{3,2,1,0:T(8,128)(2,1)S(1)}, bf16[4,2,64,384]{3,2,1,0:T(8,128)(2,1)S(1)}, u32[]{:S(2)}, u32[]{:S(2)}) collective-permute-start(bf16[4,2,64,384]{3,2,1,0:T(8,128)(2,1)S(1)} %broadcast_select_fusion.3), channel_id=1, source_target_pairs={{0,96},{4,100},{64,32},{68,36},{1,25},{5,29},{17,9},{21,13},{2,98}... | collective-permute-start | bytes 1179656 | tf_op jit(solution)/shard_map/ppermute | solution.py:427
  44.2 15.8 %collective-permute-start.16 = (bf16[4,2,64,384]{3,2,1,0:T(8,128)(2,1)S(1)}, bf16[4,2,64,384]{3,2,1,0:T(8,128)(2,1)S(1)}, u32[]{:S(2)}, u32[]{:S(2)}) collective-permute-start(bf16[4,2,64,384]{3,2,1,0:T(8,128)(2,1)S(1)} %broadcast_select_fusion.4), channel_id=1, source_target_pairs={{0,24},{4,28},{64,88},{68,92},{96,120},{100,124},{32,56},{36,60},{... | collective-permute-start | bytes 1179656 | tf_op jit(solution)/shard_map/ppermute | solution.py:427
  51.2 45.7 %collective-permute-start.19 = (bf16[15,64,384]{2,1,0:T(8,128)(2,1)}, bf16[15,64,384]{2,1,0:T(8,128)(2,1)S(1)}, u32[]{:S(2)}, u32[]{:S(2)}) collective-permute-start(bf16[15,64,384]{2,1,0:T(8,128)(2,1)} %get-tuple-element.64.own_ref), channel_id=1, source_target_pairs={{0,4},{4,8},{8,12},{12,16},{16,20},{20,24},{24,28},{28,32},{32,36}... | collective-permute-start | bytes 2211848 | tf_op jit(solution)/shard_map/ppermute | solution.py:434
  55.2 53.9 %collective-permute-start.12 = (bf16[15,64,384]{2,1,0:T(8,128)(2,1)}, bf16[15,64,384]{2,1,0:T(8,128)(2,1)}, u32[]{:S(2)}, u32[]{:S(2)}) collective-permute-start(bf16[15,64,384]{2,1,0:T(8,128)(2,1)} %get-tuple-element.60.own_ref), channel_id=1, source_target_pairs={{0,4},{4,8},{8,12},{12,16},{16,20},{20,24},{24,28},{28,32},{32,36}... | collective-permute-start | bytes 2211848 | tf_op jit(solution)/shard_map/ppermute | solution.py:434
  59.9 6.6 %collective-permute-start.8 = (bf16[4,2,64,384]{3,2,1,0:T(8,128)(2,1)S(1)}, bf16[4,2,64,384]{3,2,1,0:T(8,128)(2,1)S(1)}, u32[]{:S(2)}, u32[]{:S(2)}) collective-permute-start(bf16[4,2,64,384]{3,2,1,0:T(8,128)(2,1)S(1)} %broadcast_select_fusion.5), channel_id=1, source_target_pairs={{0,24},{4,28},{64,88},{68,92},{96,120},{100,124},{32,56},{36,60},{... | collective-permute-start | bytes 1179656 | tf_op jit(solution)/shard_map/ppermute | solution.py:427
  60.7 17.6 %collective-permute-start.17 = (bf16[4,2,64,384]{3,2,1,0:T(8,128)(2,1)S(1)}, bf16[4,2,64,384]{3,2,1,0:T(8,128)(2,1)S(1)}, u32[]{:S(2)}, u32[]{:S(2)}) collective-permute-start(bf16[4,2,64,384]{3,2,1,0:T(8,128)(2,1)S(1)} %broadcast_select_fusion.6), channel_id=1, source_target_pairs={{24,16},{28,20},{88,80},{92,84},{120,112},{124,116},{56,48},{60,52... | collective-permute-start | bytes 1179656 | tf_op jit(solution)/shard_map/ppermute | solution.py:427
  66.7 21.2 %collective-permute-start.9 = (bf16[4,2,64,384]{3,2,1,0:T(8,128)(2,1)S(1)}, bf16[4,2,64,384]{3,2,1,0:T(8,128)(2,1)S(1)}, u32[]{:S(2)}, u32[]{:S(2)}) collective-permute-start(bf16[4,2,64,384]{3,2,1,0:T(8,128)(2,1)S(1)} %broadcast_select_fusion.7), channel_id=1, source_target_pairs={{24,16},{28,20},{88,80},{92,84},{120,112},{124,116},{56,48},{60,52... | collective-permute-start | bytes 1179656 | tf_op jit(solution)/shard_map/ppermute | solution.py:427
  78.3 16.4 %collective-permute-start.18 = (bf16[4,2,64,384]{3,2,1,0:T(8,128)(2,1)S(1)}, bf16[4,2,64,384]{3,2,1,0:T(8,128)(2,1)S(1)}, u32[]{:S(2)}, u32[]{:S(2)}) collective-permute-start(bf16[4,2,64,384]{3,2,1,0:T(8,128)(2,1)S(1)} %broadcast_select_fusion.8), channel_id=1, source_target_pairs={{16,8},{20,12},{80,72},{84,76},{112,104},{116,108},{48,40},{52,44}... | collective-permute-start | bytes 1179656 | tf_op jit(solution)/shard_map/ppermute | solution.py:427
  84.6 36.5 %collective-permute-start.11 = (bf16[15,64,384]{2,1,0:T(8,128)(2,1)}, bf16[15,64,384]{2,1,0:T(8,128)(2,1)}, u32[]{:S(2)}, u32[]{:S(2)}) collective-permute-start(bf16[15,64,384]{2,1,0:T(8,128)(2,1)} %get-tuple-element.58.own_ref), channel_id=1, source_target_pairs={{0,4},{4,8},{8,12},{12,16},{16,20},{20,24},{24,28},{28,32},{32,36}... | collective-permute-start | bytes 2211848 | tf_op jit(solution)/shard_map/ppermute | solution.py:434
  87.8 44.5 %collective-permute-start.4 = (bf16[15,64,384]{2,1,0:T(8,128)(2,1)}, bf16[15,64,384]{2,1,0:T(8,128)(2,1)S(1)}, u32[]{:S(2)}, u32[]{:S(2)}) collective-permute-start(bf16[15,64,384]{2,1,0:T(8,128)(2,1)} %get-tuple-element.54.own_ref), channel_id=1, source_target_pairs={{0,4},{4,8},{8,12},{12,16},{16,20},{20,24},{24,28},{28,32},{32,36}... | collective-permute-start | bytes 2211848 | tf_op jit(solution)/shard_map/ppermute | solution.py:434
  94.7 25.6 %collective-permute-start.10 = (bf16[4,2,64,384]{3,2,1,0:T(8,128)(2,1)S(1)}, bf16[4,2,64,384]{3,2,1,0:T(8,128)(2,1)S(1)}, u32[]{:S(2)}, u32[]{:S(2)}) collective-permute-start(bf16[4,2,64,384]{3,2,1,0:T(8,128)(2,1)S(1)} %broadcast_select_fusion.9), channel_id=1, source_target_pairs={{16,8},{20,12},{80,72},{84,76},{112,104},{116,108},{48,40},{52,44}... | collective-permute-start | bytes 1179656 | tf_op jit(solution)/shard_map/ppermute | solution.py:427
  (4 other events, 4.2 us)
